TPU v7x, 128 devices: a whole 4x4x4 slice. The times are simulated.
128 devices in a mesh: row: 16 (over z, y_hi, core), col: 8 (over y_lo, x).
Axes of the slice: x: 4, y: 4 (y_hi: 2, y_lo: 2; y = y_hi * 2 + y_lo), z: 4, core: 2. Of those that a mesh axis runs over, the one named last changes fastest.
Arguments:
- layer_input: bfloat16 [2, 8192, 1024], P(None, 'row', 'col'), may hold values from -96 to 96
- out_grad: bfloat16 [2, 8192, 1024], P(None, 'row', 'col'), may hold values from -6 to 6
- token_route: int32 [2, 8192], P(None, 'row'), may hold values from 0 to 8191, as said below
- seq_lengths: int32 [2, 16, 4], P(None, 'row'), may hold values from 0 to 512, as said below
- positions: int32 [2, 8192], P(None, 'row'), may hold values from 0 to 3580, as said below
- attn_gain: bfloat16 [1024], replicated, may hold values from 0.099609375 to 1.8984375
- query_weight: bfloat16 [1024, 2048], P('row', 'col'), may hold values from -0.1875 to 0.1875
- key_weight: bfloat16 [1024, 1024], P('row', 'col'), may hold values from -0.1875 to 0.1875
- value_weight: bfloat16 [1024, 1024], P('row', 'col'), may hold values from -0.1875 to 0.1875
- query_gain: bfloat16 [128], replicated, may hold values from 0.099609375 to 1.8984375
- key_gain: bfloat16 [128], replicated, may hold values from 0.099609375 to 1.8984375
- out_weight: bfloat16 [2048, 1024], P('col', 'row'), may hold values from -0.5 to 0.5
- mlp_gain: bfloat16 [1024], replicated, may hold values from 0.099609375 to 1.8984375
- gate_weight: bfloat16 [1024, 3072], P('row', 'col'), may hold values from -0.1875 to 0.1875
- up_weight: bfloat16 [1024, 3072], P('row', 'col'), may hold values from -0.1875 to 0.1875
- down_weight: bfloat16 [3072, 1024], P('col', 'row'), may hold values from -0.109375 to 0.109375
Outputs:
- layer_output: bfloat16 [2, 8192, 1024], P(None, 'row', 'col')
- input_grad: bfloat16 [2, 8192, 1024], P(None, 'row', 'col')
- attn_gain_grad: float32 [1024], replicated
- query_grad: float32 [1024, 2048], P('row', 'col')
- key_grad: float32 [1024, 1024], P('row', 'col')
- value_grad: float32 [1024, 1024], P('row', 'col')
- query_gain_grad: float32 [128], replicated
- key_gain_grad: float32 [128], replicated
- out_proj_grad: float32 [2048, 1024], P('col', 'row')
- mlp_gain_grad: float32 [1024], replicated
- gate_grad: float32 [1024, 3072], P('row', 'col')
- up_grad: float32 [1024, 3072], P('row', 'col')
- down_grad: float32 [3072, 1024], P('col', 'row')
Inputs may be any that keep to these rules, and one draw needn't show every extreme that they name: Each row of token_route holds every number from 0 to 8191 once. Each aligned block of 512 entries holds the same number of entries of every group (g * 512 to (g + 1) * 512 - 1). `seq_lengths`: each row of 4 lengths sums to 512; nonzero lengths come first and zeros mark unused slots. Some row holds a single sequence of 512 tokens. Within each sequence of the group layout, positions rise by 1 to 3 from one token to the next.
All inputs are finite; a program needn't handle non-finite values.
Results may differ from a plain program's by a relative error of at most 0.018.
Values may be sent and summed in bfloat16 or wider, within the bound.
No kernel may reach another device: no remote copies, remote signals or barrier semaphores. Data moves between devices by JAX's collectives and lax.ppermute only.
A program may use at most 128 MiB of HBM per device.

v0:
```python
import math
import jax
import jax.numpy as jnp
from jax import lax
from jax.sharding import PartitionSpec as P

D = 1024
HEAD_SIZE = 128
EPSILON = 1e-06
ROPE_BASE = 1000000.0
NEGATIVE = -1e30
BOTH = ("row", "col")
ROWS = 16
BF = jnp.bfloat16
F32 = jnp.float32


def flat(row, col):
    return row * 8 + col


SAME_X = [[0, 1, 2, 3], [4, 5, 6, 7]]
CORES = [[2 * k, 2 * k + 1] for k in range(8)]
PLANE = [
    [flat(2 * k + core, 4 * y_lo + x) for k in range(8) for y_lo in range(2)]
    for x in range(4)
    for core in range(2)
]


def dot(a, b, dims):
    return lax.dot_general(a, b, (dims, ((), ())), preferred_element_type=F32)


def nn(a, b):
    return dot(a, b, ((1,), (0,)))


def nt(a, b):
    return dot(a, b, ((1,), (1,)))


def tn(a, b):
    return dot(a, b, ((0,), (0,)))


def exchange(blocks, axis, groups=None):
    return lax.all_to_all(blocks, axis, 0, 0, axis_index_groups=groups, tiled=True)


def rotate(t):
    half = t.shape[-1] // 2
    return jnp.concatenate([-t[..., half:], t[..., :half]], axis=-1)


def unrotate(t):
    half = t.shape[-1] // 2
    return jnp.concatenate([t[..., half:], -t[..., :half]], axis=-1)


def collect_weight(shard):
    n = shard.shape[1]
    plane = exchange(jnp.broadcast_to(shard[None], (16, 64, n)), BOTH, PLANE)
    pair = exchange(jnp.broadcast_to(plane[None], (2, 16, 64, n)), "row", CORES)
    pair = pair.reshape(2, 8, 2, 64, n)
    return jnp.transpose(pair, (1, 0, 3, 2, 4)).reshape(1024, 2, n)


def reduce_weight(grad):
    n = grad.shape[2]
    parts = jnp.transpose(grad.reshape(8, 2, 64, 2, n), (1, 0, 3, 2, 4)).astype(BF)
    parts = exchange(parts, "row", CORES)
    half = (parts[0].astype(F32) + parts[1].astype(F32)).astype(BF)
    got = exchange(half.reshape(16, 64, n), BOTH, PLANE)
    return jnp.sum(got.astype(F32), axis=0)


def send_tokens(rows):
    parts = jnp.transpose(rows.reshape(2, ROWS, 32, 128), (1, 0, 2, 3))
    parts = jnp.broadcast_to(parts[:, :, None], (ROWS, 2, 4, 32, 128)).reshape(128, 32, 128)
    got = exchange(parts, BOTH).reshape(ROWS, 8, 32, 128)
    return jnp.transpose(got, (0, 2, 1, 3)).reshape(512, 1024)


def return_tokens(part):
    parts = jnp.transpose(part.astype(BF).reshape(ROWS, 32, 8, 128), (0, 2, 1, 3))
    got = exchange(parts.reshape(128, 32, 128), BOTH).reshape(ROWS, 2, 4, 32, 128)
    total = jnp.sum(got.astype(F32), axis=2)
    return jnp.transpose(total, (1, 0, 2, 3)).reshape(2, 512, 128)


def scatter_sum(part):
    parts = jnp.transpose(part.astype(BF).reshape(512, 2, 4, 128), (2, 0, 1, 3))
    got = exchange(parts, "col", SAME_X)
    return jnp.sum(got.astype(F32), axis=0)


def collect_features(mine):
    got = exchange(jnp.broadcast_to(mine[None], (4, 512, 2, 128)), "col", SAME_X)
    return jnp.transpose(got, (1, 2, 0, 3)).reshape(512, 1024)


def body(
    layer_input,
    out_grad,
    token_route,
    seq_lengths,
    positions,
    attn_gain,
    query_weight,
    key_weight,
    value_weight,
    query_gain,
    key_gain,
    out_weight,
    mlp_gain,
    gate_weight,
    up_weight,
    down_weight,
):
    col = lax.axis_index("col")
    y_lo = col // 4
    x = col % 4
    places = jnp.arange(512, dtype=jnp.int32)
    rank = jnp.sum((token_route[:, None, :] < token_route[:, :, None]).astype(jnp.int32), axis=2)
    chosen = places[None, :, None] == rank[:, None, :]
    pick = chosen.astype(BF)
    slots_out = jnp.sum(jnp.where(chosen, (token_route % 512)[:, None, :], 0), axis=2)
    slots_all = exchange(jnp.transpose(slots_out.reshape(2, ROWS, 32), (1, 0, 2)), "row")
    slots = lax.dynamic_index_in_dim(slots_all, y_lo, 1, keepdims=False).reshape(512)

    def sort_rows(table):
        return jnp.stack([nn(pick[m], table[m]).astype(BF) for m in range(2)])

    def unsort_rows(table):
        return jnp.stack([tn(pick[m], table[m].astype(BF)).astype(BF) for m in range(2)])

    inputs = send_tokens(sort_rows(layer_input))
    grads = send_tokens(sort_rows(out_grad))
    qkv_full = collect_weight(jnp.concatenate([query_weight, key_weight, value_weight], axis=1))
    rest_full = collect_weight(
        jnp.concatenate([out_weight.T, gate_weight, up_weight, down_weight.T], axis=1)
    )
    wq, wk, wv = (qkv_full[:, :, :256], qkv_full[:, :, 256:384], qkv_full[:, :, 384:])
    wq, wk, wv = (wq.reshape(1024, 512), wk.reshape(1024, 256), wv.reshape(1024, 256))
    wo, wg, wu, wd = (
        rest_full[:, :, :256].reshape(1024, 512),
        rest_full[:, :, 256:640].reshape(1024, 768),
        rest_full[:, :, 640:1024].reshape(1024, 768),
        rest_full[:, :, 1024:].reshape(1024, 768),
    )
    gain_one = attn_gain.astype(F32)
    gain_two = mlp_gain.astype(F32)
    query_scale = query_gain.astype(F32)
    key_scale = key_gain.astype(F32)
    lengths = lax.dynamic_index_in_dim(seq_lengths, y_lo, 0, keepdims=False)[0]
    bound_one = lengths[0]
    bound_two = bound_one + lengths[1]
    bound_three = bound_two + lengths[2]
    segment = (
        (slots >= bound_one).astype(jnp.int32)
        + (slots >= bound_two).astype(jnp.int32)
        + (slots >= bound_three).astype(jnp.int32)
    )
    allowed = (segment[:, None] == segment[None, :]) & (slots[None, :] <= slots[:, None])
    my_positions = lax.dynamic_index_in_dim(positions, y_lo, 0, keepdims=False)
    position = jnp.sum(
        jnp.where(slots[:, None] == places[None, :], my_positions[None, :], 0), axis=1
    )
    freq_steps = jnp.arange(0, HEAD_SIZE, 2).astype(F32) / HEAD_SIZE
    frequency = 1.0 / ROPE_BASE**freq_steps
    angles = position.astype(F32)[:, None] * frequency[None, :]
    angles = jnp.concatenate([angles, angles], axis=-1)
    cosine, sine = (jnp.cos(angles)[:, None, :], jnp.sin(angles)[:, None, :])
    input_float = inputs.astype(F32)
    scale_one = lax.rsqrt(jnp.mean(input_float * input_float, axis=-1, keepdims=True) + EPSILON)
    hat_one = input_float * scale_one
    normed_one = (hat_one * gain_one).astype(BF)
    query_proj = nn(normed_one, wq).reshape(512, 4, HEAD_SIZE)
    key_proj = nn(normed_one, wk).reshape(512, 2, HEAD_SIZE)
    value_rows = nn(normed_one, wv).astype(BF).reshape(512, 2, HEAD_SIZE)
    query_inv = lax.rsqrt(jnp.mean(query_proj * query_proj, axis=-1, keepdims=True) + EPSILON)
    query_hat = query_proj * query_inv
    query_norm = query_hat * query_scale
    key_inv = lax.rsqrt(jnp.mean(key_proj * key_proj, axis=-1, keepdims=True) + EPSILON)
    key_hat = key_proj * key_inv
    key_norm = key_hat * key_scale
    query_rows = (query_norm * cosine + rotate(query_norm) * sine).astype(BF)
    key_rows = (key_norm * cosine + rotate(key_norm) * sine).astype(BF)
    grouped = query_rows.reshape(512, 2, 2, HEAD_SIZE)
    scores = jnp.einsum("qkrd,tkd->krqt", grouped, key_rows, preferred_element_type=F32)
    scores = jnp.where(allowed[None, None], scores * (1.0 / math.sqrt(HEAD_SIZE)), NEGATIVE)
    row_top = jnp.max(scores, axis=-1, keepdims=True)
    exp_scores = jnp.exp(scores - row_top)
    softmax = exp_scores / jnp.sum(exp_scores, axis=-1, keepdims=True)
    softmax_low = softmax.astype(BF)
    attended = jnp.einsum("krqt,tkd->qkrd", softmax_low, value_rows, preferred_element_type=F32)
    attended = attended.astype(BF).reshape(512, 512)
    summed = scatter_sum(nt(attended, wo))
    my_input = lax.dynamic_index_in_dim(inputs.reshape(512, 2, 4, 128), x, 2, keepdims=False)
    resid_mine = my_input.astype(F32) + summed
    resid = collect_features(resid_mine.astype(BF)).astype(F32)
    scale_two = lax.rsqrt(jnp.mean(resid * resid, axis=-1, keepdims=True) + EPSILON)
    hat_two = resid * scale_two
    normed_two = (hat_two * gain_two).astype(BF)
    gate = nn(normed_two, wg)
    up = nn(normed_two, wu)
    sigma = jax.nn.sigmoid(gate)
    activated = gate * sigma
    hidden = (activated * up).astype(BF)
    mine_mask = (jnp.arange(8, dtype=jnp.int32) % 4 == x).astype(F32)[None, :, None]

    def place(mine):
        wide = jnp.broadcast_to(mine[:, :, None, :], (512, 2, 4, 128)).reshape(512, 8, 128)
        return (wide * mine_mask).reshape(512, 1024)

    output_home = return_tokens(nt(hidden, wd) + place(resid_mine))
    delta_hidden = nn(grads, wd)
    delta_gate = (delta_hidden * up * sigma * (1.0 + gate * (1.0 - sigma))).astype(BF)
    delta_up = (delta_hidden * activated).astype(BF)
    delta_two = nt(delta_gate, wg) + nt(delta_up, wu)
    mlp_gain_sum = jnp.sum(delta_two * hat_two, axis=0)
    scaled = delta_two * gain_two
    inner = jnp.mean(scaled * hat_two, axis=-1, keepdims=True)
    my_grad = lax.dynamic_index_in_dim(grads.reshape(512, 2, 4, 128), x, 2, keepdims=False)
    resid_delta = my_grad.astype(F32) + scatter_sum(scale_two * (scaled - hat_two * inner))
    resid_low = collect_features(resid_delta.astype(BF))
    delta_attended = nn(resid_low, wo).astype(BF).reshape(512, 2, 2, HEAD_SIZE)
    rest_grad = jnp.concatenate(
        [
            tn(resid_low, attended).reshape(1024, 2, 256),
            tn(normed_two, delta_gate).reshape(1024, 2, 384),
            tn(normed_two, delta_up).reshape(1024, 2, 384),
            tn(grads, hidden).reshape(1024, 2, 384),
        ],
        axis=2,
    )
    rest_total = reduce_weight(rest_grad)
    delta_probs = jnp.einsum(
        "qkrd,tkd->krqt", delta_attended, value_rows, preferred_element_type=F32
    )
    delta_value = jnp.einsum(
        "krqt,qkrd->tkd", softmax_low, delta_attended, preferred_element_type=F32
    )
    delta_scores = (
        softmax * (delta_probs - jnp.sum(delta_probs * softmax, axis=-1, keepdims=True))
    ).astype(BF)
    delta_query = jnp.einsum(
        "krqt,tkd->qkrd", delta_scores, key_rows, preferred_element_type=F32
    ) * (1.0 / math.sqrt(HEAD_SIZE))
    delta_key = jnp.einsum("krqt,qkrd->tkd", delta_scores, grouped, preferred_element_type=F32) * (
        1.0 / math.sqrt(HEAD_SIZE)
    )
    delta_query = delta_query.reshape(512, 4, HEAD_SIZE)
    delta_query_norm = delta_query * cosine + unrotate(delta_query * sine)
    delta_key_norm = delta_key * cosine + unrotate(delta_key * sine)
    query_gain_sum = jnp.sum(delta_query_norm * query_hat, axis=(0, 1))
    key_gain_sum = jnp.sum(delta_key_norm * key_hat, axis=(0, 1))

    def norm_back(delta, hat, inv, gain):
        part = delta * gain
        part = inv * (part - hat * jnp.mean(part * hat, axis=-1, keepdims=True))
        return part.astype(BF).reshape(512, -1)

    delta_query_proj = norm_back(delta_query_norm, query_hat, query_inv, query_scale)
    delta_key_proj = norm_back(delta_key_norm, key_hat, key_inv, key_scale)
    delta_value_proj = delta_value.astype(BF).reshape(512, -1)
    delta_one = nt(delta_query_proj, wq) + nt(delta_key_proj, wk) + nt(delta_value_proj, wv)
    attn_gain_sum = jnp.sum(delta_one * hat_one, axis=0)
    scaled = delta_one * gain_one
    inner = jnp.mean(scaled * hat_one, axis=-1, keepdims=True)
    delta_home = return_tokens(scale_one * (scaled - hat_one * inner) + place(resid_delta))
    qkv_grad = jnp.concatenate(
        [
            tn(normed_one, delta_query_proj).reshape(1024, 2, 256),
            tn(normed_one, delta_key_proj).reshape(1024, 2, 128),
            tn(normed_one, delta_value_proj).reshape(1024, 2, 128),
        ],
        axis=2,
    )
    qkv_total = reduce_weight(qkv_grad)
    attn_gain_grad, mlp_gain_grad, query_gain_grad, key_gain_grad = lax.psum(
        (attn_gain_sum, mlp_gain_sum, query_gain_sum, key_gain_sum), BOTH
    )
    return (
        unsort_rows(output_home),
        unsort_rows(delta_home),
        attn_gain_grad,
        qkv_total[:, :256],
        qkv_total[:, 256:384],
        qkv_total[:, 384:],
        query_gain_grad,
        key_gain_grad,
        rest_total[:, :256].T,
        mlp_gain_grad,
        rest_total[:, 256:640],
        rest_total[:, 640:1024],
        rest_total[:, 1024:].T,
    )


def solution(mesh):
    in_specs = (
        P(None, "row", "col"),
        P(None, "row", "col"),
        P(None, "row"),
        P(None, "row", None),
        P(None, "row"),
        P(),
        P("row", "col"),
        P("row", "col"),
        P("row", "col"),
        P(),
        P(),
        P("col", "row"),
        P(),
        P("row", "col"),
        P("row", "col"),
        P("col", "row"),
    )
    out_specs = (
        P(None, "row", "col"),
        P(None, "row", "col"),
        P(),
        P("row", "col"),
        P("row", "col"),
        P("row", "col"),
        P(),
        P(),
        P("col", "row"),
        P(),
        P("row", "col"),
        P("row", "col"),
        P("col", "row"),
    )
    return jax.shard_map(body, mesh=mesh, in_specs=in_specs, out_specs=out_specs, check_vma=False)
```

profile of v0, /device:TPU:1, one launch (start us, length us, event | category | flops | bytes accessed | tf_op | source)
XLA Modules:
  0.0 547.3 jit_solution(2396641583294308032)
XLA Ops:
  3.5 9.5 %all-to-all-start.3 = ((s32[16,2,32]{2,1,0:T(2,128)}), s32[16,2,32]{2,1,0:T(2,128)S(1)}, u32[]{:S(2)}, u32[]{:S(2)}) async-start(s32[16,2,32]{2,1,0:T(2,128)} %copy.266), calls=%async_computation.3 | async-start | bytes 32768 | tf_op jit(solution)/shard_map/all_to_all | solution.py:48
  29.6 12.3 %all-to-all-done.1 = bf16[16,64,512]{2,1,0:T(8,128)(2,1)S(1)} async-done(((bf16[16,64,512]{2,1,0:T(8,128)(2,1)}), bf16[16,64,512]{2,1,0:T(8,128)(2,1)S(1)}, u32[]{:S(2)}, u32[]{:S(2)}) %all-to-all-start.1) | async-done | bytes 1048608 | tf_op jit(solution)/shard_map/all_to_all | solution.py:48
  42.1 6.9 %all_to_all.85 = bf16[2,16,64,512]{3,2,1,0:T(8,128)(2,1)S(1)} all-to-all(bf16[2,16,64,512]{3,2,1,0:T(8,128)(2,1)S(1)} %broadcast_in_dim.60), channel_id=1, replica_groups={{0,8},{16,24},{32,40},{48,56},{64,72},{80,88},{96,104},{112,120},{1,9},..., dimensions={0} | all-to-all | bytes 4194304 | tf_op jit(solution)/shard_map/all_to_all | solution.py:48
  50.2 5.5 all-to-all-start
  64.1 11.0 %all-to-all-done = bf16[128,32,128]{2,1,0:T(8,128)(2,1)S(1)} async-done(((bf16[128,32,128]{2,1,0:T(8,128)(2,1)}), bf16[128,32,128]{2,1,0:T(8,128)(2,1)S(1)}, u32[]{:S(2)}, u32[]{:S(2)}) %all-to-all-start) | async-done | bytes 1048608 | tf_op jit(solution)/shard_map/all_to_all | solution.py:48
  77.0 4.7 all-to-all-start.4
  92.9 31.9 %all-to-all-done.4 = bf16[16,64,1408]{2,1,0:T(8,128)(2,1)} async-done(((bf16[16,64,1408]{2,1,0:T(8,128)(2,1)}), bf16[16,64,1408]{2,1,0:T(8,128)(2,1)}, u32[]{:S(2)}, u32[]{:S(2)}) %all-to-all-start.4) | async-done | bytes 2883616 | tf_op jit(solution)/shard_map/all_to_all | solution.py:48
  127.4 10.9 %all_to_all.86 = bf16[2,16,64,1408]{3,2,1,0:T(8,128)(2,1)} all-to-all(bf16[2,16,64,1408]{3,2,1,0:T(8,128)(2,1)S(1)} %broadcast_in_dim.73), channel_id=1, replica_groups={{0,8},{16,24},{32,40},{48,56},{64,72},{80,88},{96,104},{112,120},{1,9},..., dimensions={0} | all-to-all | bytes 11534336 | tf_op jit(solution)/shard_map/all_to_all | solution.py:48
  139.4 5.6 %all-to-all-start.9 = ((bf16[128,32,128]{2,1,0:T(8,128)(2,1)}), bf16[128,32,128]{2,1,0:T(8,128)(2,1)S(1)}, u32[]{:S(2)}, u32[]{:S(2)}) async-start(bf16[128,32,128]{2,1,0:T(8,128)(2,1)} %bitcast.399), calls=%async_computation.9 | async-start | bytes 2097152 | tf_op jit(solution)/shard_map/all_to_all | solution.py:48
  189.4 4.7 all-to-all-start.7
  194.2 4.6 fusion.73
  245.0 4.4 all-to-all-start.10
  304.8 4.6 fusion.3
  325.4 9.3 %all-to-all-start.13 = ((bf16[2,8,2,64,512]{4,3,1,2,0:T(8,128)(2,1)}), bf16[2,8,2,64,512]{4,3,1,2,0:T(8,128)(2,1)}, u32[]{:S(2)}, u32[]{:S(2)}) async-start(bf16[2,8,2,64,512]{4,3,1,2,0:T(8,128)(2,1)} %copy.301), calls=%async_computation.13 | async-start | bytes 4194304 | tf_op jit(solution)/shard_map/all_to_all | solution.py:48
  336.6 5.1 pad_maximum_fusion
  341.6 8.4 %all-to-all-start.8 = ((bf16[128,32,128]{2,1,0:T(8,128)(2,1)}), bf16[128,32,128]{2,1,0:T(8,128)(2,1)S(1)}, u32[]{:S(2)}, u32[]{:S(2)}) async-start(bf16[128,32,128]{2,1,0:T(8,128)(2,1)} %bitcast.400), calls=%async_computation.8 | async-start | bytes 2097152 | tf_op jit(solution)/shard_map/all_to_all | solution.py:48
  353.0 8.3 %copy.309 = bf16[1024,2,1408]{2,0,1:T(8,128)(2,1)} copy(bf16[1024,2,1408]{0,2,1:T(8,128)(2,1)} %pad_maximum_fusion) | data formatting | bytes 11534336 | tf_op jit(solution)/shard_map/concatenate | solution.py:229
  361.3 5.7 %copy.310 = bf16[2,8,2,64,1408]{4,3,1,2,0:T(8,128)(2,1)} copy(bf16[2,8,2,64,1408]{4,3,0,1,2:T(8,128)(2,1)} %bitcast.384) | data formatting | bytes 11534336 | tf_op jit(solution)/shard_map/convert_element_type | solution.py:71
  372.4 15.2 %all_to_all.87 = bf16[2,8,2,64,1408]{4,3,1,2,0:T(8,128)(2,1)} all-to-all(bf16[2,8,2,64,1408]{4,3,1,2,0:T(8,128)(2,1)} %copy.310), channel_id=1, replica_groups={{0,8},{16,24},{32,40},{48,56},{64,72},{80,88},{96,104},{112,120},{1,9},..., dimensions={0} | all-to-all | bytes 11534336 | tf_op jit(solution)/shard_map/all_to_all | solution.py:48
  387.6 6.9 %all-to-all-start.14 = ((bf16[16,64,512]{2,1,0:T(8,128)(2,1)}), bf16[16,64,512]{2,1,0:T(8,128)(2,1)S(1)}, u32[]{:S(2)}, u32[]{:S(2)}) async-start(bf16[16,64,512]{2,1,0:T(8,128)(2,1)} %bitcast.114), calls=%async_computation.14 | async-start | bytes 2097152 | tf_op jit(solution)/shard_map/all_to_all | solution.py:48
  400.8 10.0 %all-to-all-done.14 = bf16[16,64,512]{2,1,0:T(8,128)(2,1)S(1)} async-done(((bf16[16,64,512]{2,1,0:T(8,128)(2,1)}), bf16[16,64,512]{2,1,0:T(8,128)(2,1)S(1)}, u32[]{:S(2)}, u32[]{:S(2)}) %all-to-all-start.14) | async-done | bytes 1048608 | tf_op jit(solution)/shard_map/all_to_all | solution.py:48
  410.8 7.2 %all-to-all-start.12 = ((bf16[128,32,128]{2,1,0:T(8,128)(2,1)}), bf16[128,32,128]{2,1,0:T(8,128)(2,1)S(1)}, u32[]{:S(2)}, u32[]{:S(2)}) async-start(bf16[128,32,128]{2,1,0:T(8,128)(2,1)} %bitcast.97), calls=%async_computation.12 | async-start | bytes 2097152 | tf_op jit(solution)/shard_map/all_to_all | solution.py:48
  423.6 13.8 %all-to-all-done.12 = bf16[128,32,128]{2,1,0:T(8,128)(2,1)S(1)} async-done(((bf16[128,32,128]{2,1,0:T(8,128)(2,1)}), bf16[128,32,128]{2,1,0:T(8,128)(2,1)S(1)}, u32[]{:S(2)}, u32[]{:S(2)}) %all-to-all-start.12) | async-done | bytes 1048608 | tf_op jit(solution)/shard_map/all_to_all | solution.py:48
  445.4 94.9 %all-reduce = (f32[1024]{0:T(1024)}, f32[128]{0:T(128)}, f32[128]{0:T(128)}, f32[1024]{0:T(1024)}) all-reduce(f32[1024]{0:T(1024)S(1)} %get-tuple-element.15, f32[128]{0:T(128)S(1)} %get-tuple-element.17, f32[128]{0:T(128)S(1)} %get-tuple-element.19, f32[1024]{0:T(1024)S(1)} %get-tuple-element.13), channel_id=1, replica_groups=mesh['row'=16,'col'=8] {'row','col'}, use_global_device_ids=true, to_apply=%region_19.20 | all-reduce | flops 2304 | bytes 18432 | tf_op jit(solution)/shard_map/psum | solution.py:282
  (320 shorter events, 241.4 us)
Async XLA Ops:
  0.6 27.8 %copy-start = (s32[2,512]{1,0:T(2,128)S(1)}, s32[2,512]{1,0:T(2,128)}, u32[]{:S(2)}) copy-start(s32[2,512]{1,0:T(2,128)} %param.20) | copy-start | bytes 12292
  0.7 15.4 %copy-start.58 = (bf16[2,512,128]{2,1,0:T(8,128)(2,1)S(1)}, bf16[2,512,128]{2,1,0:T(8,128)(2,1)}, u32[]{:S(2)}) copy-start(bf16[2,512,128]{2,1,0:T(8,128)(2,1)} %param.17) | copy-start | bytes 786436
  3.5 16.8 %all-to-all-start.3 = ((s32[16,2,32]{2,1,0:T(2,128)}), s32[16,2,32]{2,1,0:T(2,128)S(1)}, u32[]{:S(2)}, u32[]{:S(2)}) async-start(s32[16,2,32]{2,1,0:T(2,128)} %copy.266), calls=%async_computation.3 | async-start | bytes 32768 | tf_op jit(solution)/shard_map/all_to_all | solution.py:48
  16.9 11.6 %copy-start.56 = (bf16[1024]{0:T(1024)(128)(2,1)S(1)}, bf16[1024]{0:T(1024)(128)(2,1)}, u32[]{:S(2)}) copy-start(bf16[1024]{0:T(1024)(128)(2,1)} %param.21) | copy-start | bytes 6148
  16.9 11.6 %copy-start.49 = (bf16[384,64]{0,1:T(8,128)(2,1)S(1)}, bf16[384,64]{0,1:T(8,128)(2,1)}, u32[]{:S(2)}) copy-start(bf16[384,64]{0,1:T(8,128)(2,1)} %param.31) | copy-start | bytes 147460
  16.9 11.6 %copy-start.50 = (bf16[64,384]{1,0:T(8,128)(2,1)S(1)}, bf16[64,384]{1,0:T(8,128)(2,1)}, u32[]{:S(2)}) copy-start(bf16[64,384]{1,0:T(8,128)(2,1)} %param.30) | copy-start | bytes 147460
  16.9 11.6 %copy-start.51 = (bf16[64,384]{1,0:T(8,128)(2,1)S(1)}, bf16[64,384]{1,0:T(8,128)(2,1)}, u32[]{:S(2)}) copy-start(bf16[64,384]{1,0:T(8,128)(2,1)} %param.29) | copy-start | bytes 147460
  17.0 11.6 %copy-start.53 = (bf16[256,64]{0,1:T(8,128)(2,1)S(1)}, bf16[256,64]{0,1:T(8,128)(2,1)}, u32[]{:S(2)}) copy-start(bf16[256,64]{0,1:T(8,128)(2,1)} %param.27) | copy-start | bytes 98308
  21.4 20.5 %all-to-all-start.1 = ((bf16[16,64,512]{2,1,0:T(8,128)(2,1)}), bf16[16,64,512]{2,1,0:T(8,128)(2,1)S(1)}, u32[]{:S(2)}, u32[]{:S(2)}) async-start(bf16[16,64,512]{2,1,0:T(8,128)(2,1)} %broadcast_in_dim.59), calls=%async_computation.1 | async-start | bytes 2097152 | tf_op jit(solution)/shard_map/all_to_all | solution.py:48
  50.2 24.9 %all-to-all-start = ((bf16[128,32,128]{2,1,0:T(8,128)(2,1)}), bf16[128,32,128]{2,1,0:T(8,128)(2,1)S(1)}, u32[]{:S(2)}, u32[]{:S(2)}) async-start(bf16[128,32,128]{2,1,0:T(8,128)(2,1)} %bitcast.398), calls=%async_computation | async-start | bytes 2097152 | tf_op jit(solution)/shard_map/all_to_all | solution.py:48
  61.7 13.3 %copy-start.44 = (bf16[64,1408]{1,0:T(8,128)(2,1)S(1)}, bf16[64,1408]{1,0:T(8,128)(2,1)}, u32[]{:S(2)}) copy-start(bf16[64,1408]{1,0:T(8,128)(2,1)} %pad_maximum_fusion.5) | copy-start | bytes 540676
  77.0 47.9 %all-to-all-start.4 = ((bf16[16,64,1408]{2,1,0:T(8,128)(2,1)}), bf16[16,64,1408]{2,1,0:T(8,128)(2,1)}, u32[]{:S(2)}, u32[]{:S(2)}) async-start(bf16[16,64,1408]{2,1,0:T(8,128)(2,1)} %broadcast_in_dim.72), calls=%async_computation.4 | async-start | bytes 5767168 | tf_op jit(solution)/shard_map/all_to_all | solution.py:48
  127.4 10.9 %copy-start.37 = (bf16[16,2,32,128]{3,2,1,0:T(8,128)(2,1)S(1)}, bf16[16,2,32,128]{3,2,1,0:T(8,128)(2,1)}, u32[]{:S(2)}) copy-start(bf16[16,2,32,128]{3,2,1,0:T(8,128)(2,1)} %copy.282) | copy-start | bytes 786436
  139.4 26.4 %all-to-all-start.9 = ((bf16[128,32,128]{2,1,0:T(8,128)(2,1)}), bf16[128,32,128]{2,1,0:T(8,128)(2,1)S(1)}, u32[]{:S(2)}, u32[]{:S(2)}) async-start(bf16[128,32,128]{2,1,0:T(8,128)(2,1)} %bitcast.399), calls=%async_computation.9 | async-start | bytes 2097152 | tf_op jit(solution)/shard_map/all_to_all | solution.py:48
  165.8 18.4 %all-to-all-start.6 = ((bf16[4,512,2,128]{3,2,1,0:T(2,128)(2,1)}), bf16[4,512,2,128]{3,2,1,0:T(2,128)(2,1)}, u32[]{:S(2)}, u32[]{:S(2)}) async-start(bf16[4,512,2,128]{3,2,1,0:T(2,128)(2,1)} %bitcast.403), calls=%async_computation.6 | async-start | bytes 2097152 | tf_op jit(solution)/shard_map/all_to_all | solution.py:48
  189.4 26.5 %all-to-all-start.7 = ((bf16[4,512,2,128]{3,2,1,0:T(2,128)(2,1)}), bf16[4,512,2,128]{3,2,1,0:T(2,128)(2,1)}, u32[]{:S(2)}, u32[]{:S(2)}) async-start(bf16[4,512,2,128]{3,2,1,0:T(2,128)(2,1)} %broadcast_in_dim.74), calls=%async_computation.7 | async-start | bytes 2097152 | tf_op jit(solution)/shard_map/all_to_all | solution.py:48
  245.0 20.6 %all-to-all-start.10 = ((bf16[4,512,2,128]{3,2,1,0:T(2,128)(2,1)}), bf16[4,512,2,128]{3,2,1,0:T(2,128)(2,1)}, u32[]{:S(2)}, u32[]{:S(2)}) async-start(bf16[4,512,2,128]{3,2,1,0:T(2,128)(2,1)} %bitcast.404), calls=%async_computation.10 | async-start | bytes 2097152 | tf_op jit(solution)/shard_map/all_to_all | solution.py:48
  270.8 16.1 %all-to-all-start.11 = ((bf16[4,512,2,128]{3,2,1,0:T(2,128)(2,1)}), bf16[4,512,2,128]{3,2,1,0:T(2,128)(2,1)}, u32[]{:S(2)}, u32[]{:S(2)}) async-start(bf16[4,512,2,128]{3,2,1,0:T(2,128)(2,1)} %broadcast_in_dim.78), calls=%async_computation.11 | async-start | bytes 2097152 | tf_op jit(solution)/shard_map/all_to_all | solution.py:48
  325.4 16.2 %all-to-all-start.13 = ((bf16[2,8,2,64,512]{4,3,1,2,0:T(8,128)(2,1)}), bf16[2,8,2,64,512]{4,3,1,2,0:T(8,128)(2,1)}, u32[]{:S(2)}, u32[]{:S(2)}) async-start(bf16[2,8,2,64,512]{4,3,1,2,0:T(8,128)(2,1)} %copy.301), calls=%async_computation.13 | async-start | bytes 4194304 | tf_op jit(solution)/shard_map/all_to_all | solution.py:48
  341.6 30.7 %all-to-all-start.8 = ((bf16[128,32,128]{2,1,0:T(8,128)(2,1)}), bf16[128,32,128]{2,1,0:T(8,128)(2,1)S(1)}, u32[]{:S(2)}, u32[]{:S(2)}) async-start(bf16[128,32,128]{2,1,0:T(8,128)(2,1)} %bitcast.400), calls=%async_computation.8 | async-start | bytes 2097152 | tf_op jit(solution)/shard_map/all_to_all | solution.py:48
  372.4 15.2 %copy-start.17 = (bf16[128,32,128]{2,1,0:T(8,128)(2,1)}, bf16[128,32,128]{2,1,0:T(8,128)(2,1)S(1)}, u32[]{:S(2)}) copy-start(bf16[128,32,128]{2,1,0:T(8,128)(2,1)S(1)} %all-to-all-done.8) | copy-start | bytes 3145732
  387.6 23.2 %all-to-all-start.14 = ((bf16[16,64,512]{2,1,0:T(8,128)(2,1)}), bf16[16,64,512]{2,1,0:T(8,128)(2,1)S(1)}, u32[]{:S(2)}, u32[]{:S(2)}) async-start(bf16[16,64,512]{2,1,0:T(8,128)(2,1)} %bitcast.114), calls=%async_computation.14 | async-start | bytes 2097152 | tf_op jit(solution)/shard_map/all_to_all | solution.py:48
  410.8 26.6 %all-to-all-start.12 = ((bf16[128,32,128]{2,1,0:T(8,128)(2,1)}), bf16[128,32,128]{2,1,0:T(8,128)(2,1)S(1)}, u32[]{:S(2)}, u32[]{:S(2)}) async-start(bf16[128,32,128]{2,1,0:T(8,128)(2,1)} %bitcast.97), calls=%async_computation.12 | async-start | bytes 2097152 | tf_op jit(solution)/shard_map/all_to_all | solution.py:48
  438.5 106.6 %all-to-all-start.16 = ((bf16[16,64,1408]{2,1,0:T(8,128)(2,1)}), bf16[16,64,1408]{2,1,0:T(8,128)(2,1)S(1)}, u32[]{:S(2)}, u32[]{:S(2)}) async-start(bf16[16,64,1408]{2,1,0:T(8,128)(2,1)} %bitcast.128), calls=%async_computation.16 | async-start | bytes 5767168 | tf_op jit(solution)/shard_map/all_to_all | solution.py:48
  (59 other events, 182.7 us)
where the time goes:
time: 556 us; the launch traced here: 547 us
  local copies, waits for them, and re-layouts  134 us (24%)
  blocking collectives  128 us (23%)
  waiting for transfers between devices  85.7 us (15%)
  starting transfers between devices  82.1 us (15%)
  matrix products  68.2 us (12%)
  other arithmetic  45.3 us (8%)
    psum x1, blocking collectives, body(): lax.psum((attn_gain_sum, mlp_gain_sum, query_gain_sum, key_gain_sum), BOTH)  94.9 us
    all_to_all x14, waiting for transfers between devices, exchange(): lax.all_to_all(blocks, axis, 0, 0, axis_index_groups=groups, tiled=True)  85.7 us
    all_to_all x14, starting transfers between devices, exchange(): lax.all_to_all(blocks, axis, 0, 0, axis_index_groups=groups, tiled=True)  82.1 us
    dot_general x29, matrix products, dot(): return lax.dot_general(a, b, (dims, ((), ())), preferred_element_type=F32)  53 us
    all_to_all x3, blocking collectives, exchange(): lax.all_to_all(blocks, axis, 0, 0, axis_index_groups=groups, tiled=True)  33 us
    unnamed x140, local copies, waits for them, and re-layouts  13.9 us
    reshape x4, local copies, waits for them, and re-layouts, scatter_sum(): parts = jnp.transpose(part.astype(BF).reshape(512, 2, 4, 128), (2, 0, 1, 3))  11.2 us
  transfers between devices with their start and end apart: 14, of which 8 were waited for; matrix products, arithmetic and copies ran while one was open for 27% of the time, Pallas kernels for 0%

commit v1 on v0

--- a/solution.py
+++ b/solution.py
@@ -280,7 +280,7 @@
     )
     qkv_total = reduce_weight(qkv_grad)
     attn_gain_grad, mlp_gain_grad, query_gain_grad, key_gain_grad = lax.psum(
-        (attn_gain_sum, mlp_gain_sum, query_gain_sum, key_gain_sum), BOTH
+        lax.psum((attn_gain_sum, mlp_gain_sum, query_gain_sum, key_gain_sum), "col"), "row"
     )
     return (
         unsort_rows(output_home),

time: 556 us -> 530 us (0.953)
  the two profiles are of different devices: /device:TPU:1 before, /device:TPU:8 now
where the time goes in v1:
time: 530 us; the launch traced here: 521 us
  local copies, waits for them, and re-layouts  132 us (25%)
  blocking collectives  99 us (19%)
  starting transfers between devices  88.6 us (17%)
  waiting for transfers between devices  82.2 us (16%)
  matrix products  68.1 us (13%)
  other arithmetic  46.3 us (9%)
    all_to_all x14, starting transfers between devices, exchange(): lax.all_to_all(blocks, axis, 0, 0, axis_index_groups=groups, tiled=True)  88.6 us
    all_to_all x14, waiting for transfers between devices, exchange(): lax.all_to_all(blocks, axis, 0, 0, axis_index_groups=groups, tiled=True)  82.2 us
    dot_general x29, matrix products, dot(): return lax.dot_general(a, b, (dims, ((), ())), preferred_element_type=F32)  53 us
    psum x1, blocking collectives, body(): lax.psum(lax.psum((attn_gain_sum, mlp_gain_sum, query_gain_sum, key_gain_...  51.3 us
    all_to_all x3, blocking collectives, exchange(): lax.all_to_all(blocks, axis, 0, 0, axis_index_groups=groups, tiled=True)  29.6 us
    psum x1, blocking collectives, body(): lax.psum((attn_gain_sum, mlp_gain_sum, query_gain_sum, key_gain_sum), 'col')  18.1 us
    unnamed x140, local copies, waits for them, and re-layouts  12.8 us
    reshape x4, local copies, waits for them, and re-layouts, scatter_sum(): parts = jnp.transpose(part.astype(BF).reshape(512, 2, 4, 128), (2, 0, 1, 3))  11.2 us
  transfers between devices with their start and end apart: 14, of which 8 were waited for; matrix products, arithmetic and copies ran while one was open for 29% of the time, Pallas kernels for 0%

profile of v1, /device:TPU:8, one launch (start us, length us, event | category | flops | bytes accessed | tf_op | source)
XLA Modules:
  0.0 521.0 jit_solution(5941026349492683290)
XLA Ops:
  3.5 7.1 %all-to-all-start.3 = ((s32[16,2,32]{2,1,0:T(2,128)}), s32[16,2,32]{2,1,0:T(2,128)S(1)}, u32[]{:S(2)}, u32[]{:S(2)}) async-start(s32[16,2,32]{2,1,0:T(2,128)} %copy.266), calls=%async_computation.3 | async-start | bytes 32768 | tf_op jit(solution)/shard_map/all_to_all | solution.py:48
  19.4 4.9 all-to-all-start.1
  28.8 11.8 %all-to-all-done.1 = bf16[16,64,512]{2,1,0:T(8,128)(2,1)S(1)} async-done(((bf16[16,64,512]{2,1,0:T(8,128)(2,1)}), bf16[16,64,512]{2,1,0:T(8,128)(2,1)S(1)}, u32[]{:S(2)}, u32[]{:S(2)}) %all-to-all-start.1) | async-done | bytes 1048608 | tf_op jit(solution)/shard_map/all_to_all | solution.py:48
  40.9 5.4 %all_to_all.85 = bf16[2,16,64,512]{3,2,1,0:T(8,128)(2,1)S(1)} all-to-all(bf16[2,16,64,512]{3,2,1,0:T(8,128)(2,1)S(1)} %broadcast_in_dim.60), channel_id=1, replica_groups={{0,8},{16,24},{32,40},{48,56},{64,72},{80,88},{96,104},{112,120},{1,9},..., dimensions={0} | all-to-all | bytes 4194304 | tf_op jit(solution)/shard_map/all_to_all | solution.py:48
  47.4 7.2 %all-to-all-start = ((bf16[128,32,128]{2,1,0:T(8,128)(2,1)}), bf16[128,32,128]{2,1,0:T(8,128)(2,1)S(1)}, u32[]{:S(2)}, u32[]{:S(2)}) async-start(bf16[128,32,128]{2,1,0:T(8,128)(2,1)} %bitcast.398), calls=%async_computation | async-start | bytes 2097152 | tf_op jit(solution)/shard_map/all_to_all | solution.py:48
  63.0 9.5 %all-to-all-done = bf16[128,32,128]{2,1,0:T(8,128)(2,1)S(1)} async-done(((bf16[128,32,128]{2,1,0:T(8,128)(2,1)}), bf16[128,32,128]{2,1,0:T(8,128)(2,1)S(1)}, u32[]{:S(2)}, u32[]{:S(2)}) %all-to-all-start) | async-done | bytes 1048608 | tf_op jit(solution)/shard_map/all_to_all | solution.py:48
  74.4 6.9 %all-to-all-start.4 = ((bf16[16,64,1408]{2,1,0:T(8,128)(2,1)}), bf16[16,64,1408]{2,1,0:T(8,128)(2,1)}, u32[]{:S(2)}, u32[]{:S(2)}) async-start(bf16[16,64,1408]{2,1,0:T(8,128)(2,1)} %broadcast_in_dim.72), calls=%async_computation.4 | async-start | bytes 5767168 | tf_op jit(solution)/shard_map/all_to_all | solution.py:48
  92.6 28.2 %all-to-all-done.4 = bf16[16,64,1408]{2,1,0:T(8,128)(2,1)} async-done(((bf16[16,64,1408]{2,1,0:T(8,128)(2,1)}), bf16[16,64,1408]{2,1,0:T(8,128)(2,1)}, u32[]{:S(2)}, u32[]{:S(2)}) %all-to-all-start.4) | async-done | bytes 2883616 | tf_op jit(solution)/shard_map/all_to_all | solution.py:48
  123.3 9.6 %all_to_all.86 = bf16[2,16,64,1408]{3,2,1,0:T(8,128)(2,1)} all-to-all(bf16[2,16,64,1408]{3,2,1,0:T(8,128)(2,1)S(1)} %broadcast_in_dim.73), channel_id=1, replica_groups={{0,8},{16,24},{32,40},{48,56},{64,72},{80,88},{96,104},{112,120},{1,9},..., dimensions={0} | all-to-all | bytes 11534336 | tf_op jit(solution)/shard_map/all_to_all | solution.py:48
  134.1 9.9 %all-to-all-start.9 = ((bf16[128,32,128]{2,1,0:T(8,128)(2,1)}), bf16[128,32,128]{2,1,0:T(8,128)(2,1)S(1)}, u32[]{:S(2)}, u32[]{:S(2)}) async-start(bf16[128,32,128]{2,1,0:T(8,128)(2,1)} %bitcast.399), calls=%async_computation.9 | async-start | bytes 2097152 | tf_op jit(solution)/shard_map/all_to_all | solution.py:48
  245.4 4.9 all-to-all-start.10
  328.8 4.9 all-to-all-start.13
  335.6 5.0 pad_maximum_fusion
  340.7 8.0 %all-to-all-start.8 = ((bf16[128,32,128]{2,1,0:T(8,128)(2,1)}), bf16[128,32,128]{2,1,0:T(8,128)(2,1)S(1)}, u32[]{:S(2)}, u32[]{:S(2)}) async-start(bf16[128,32,128]{2,1,0:T(8,128)(2,1)} %bitcast.400), calls=%async_computation.8 | async-start | bytes 2097152 | tf_op jit(solution)/shard_map/all_to_all | solution.py:48
  351.5 8.3 %copy.309 = bf16[1024,2,1408]{2,0,1:T(8,128)(2,1)} copy(bf16[1024,2,1408]{0,2,1:T(8,128)(2,1)} %pad_maximum_fusion) | data formatting | bytes 11534336 | tf_op jit(solution)/shard_map/concatenate | solution.py:229
  359.9 5.7 %copy.310 = bf16[2,8,2,64,1408]{4,3,1,2,0:T(8,128)(2,1)} copy(bf16[2,8,2,64,1408]{4,3,0,1,2:T(8,128)(2,1)} %bitcast.384) | data formatting | bytes 11534336 | tf_op jit(solution)/shard_map/convert_element_type | solution.py:71
  370.9 14.6 %all_to_all.87 = bf16[2,8,2,64,1408]{4,3,1,2,0:T(8,128)(2,1)} all-to-all(bf16[2,8,2,64,1408]{4,3,1,2,0:T(8,128)(2,1)} %copy.310), channel_id=1, replica_groups={{0,8},{16,24},{32,40},{48,56},{64,72},{80,88},{96,104},{112,120},{1,9},..., dimensions={0} | all-to-all | bytes 11534336 | tf_op jit(solution)/shard_map/all_to_all | solution.py:48
  385.5 8.2 %all-to-all-start.14 = ((bf16[16,64,512]{2,1,0:T(8,128)(2,1)}), bf16[16,64,512]{2,1,0:T(8,128)(2,1)S(1)}, u32[]{:S(2)}, u32[]{:S(2)}) async-start(bf16[16,64,512]{2,1,0:T(8,128)(2,1)} %bitcast.114), calls=%async_computation.14 | async-start | bytes 2097152 | tf_op jit(solution)/shard_map/all_to_all | solution.py:48
  400.0 9.7 %all-to-all-done.14 = bf16[16,64,512]{2,1,0:T(8,128)(2,1)S(1)} async-done(((bf16[16,64,512]{2,1,0:T(8,128)(2,1)}), bf16[16,64,512]{2,1,0:T(8,128)(2,1)S(1)}, u32[]{:S(2)}, u32[]{:S(2)}) %all-to-all-start.14) | async-done | bytes 1048608 | tf_op jit(solution)/shard_map/all_to_all | solution.py:48
  409.7 6.9 %all-to-all-start.12 = ((bf16[128,32,128]{2,1,0:T(8,128)(2,1)}), bf16[128,32,128]{2,1,0:T(8,128)(2,1)S(1)}, u32[]{:S(2)}, u32[]{:S(2)}) async-start(bf16[128,32,128]{2,1,0:T(8,128)(2,1)} %bitcast.97), calls=%async_computation.12 | async-start | bytes 2097152 | tf_op jit(solution)/shard_map/all_to_all | solution.py:48
  422.2 12.3 %all-to-all-done.12 = bf16[128,32,128]{2,1,0:T(8,128)(2,1)S(1)} async-done(((bf16[128,32,128]{2,1,0:T(8,128)(2,1)}), bf16[128,32,128]{2,1,0:T(8,128)(2,1)S(1)}, u32[]{:S(2)}, u32[]{:S(2)}) %all-to-all-start.12) | async-done | bytes 1048608 | tf_op jit(solution)/shard_map/all_to_all | solution.py:48
  435.5 5.8 %all-to-all-start.16 = ((bf16[16,64,1408]{2,1,0:T(8,128)(2,1)}), bf16[16,64,1408]{2,1,0:T(8,128)(2,1)S(1)}, u32[]{:S(2)}, u32[]{:S(2)}) async-start(bf16[16,64,1408]{2,1,0:T(8,128)(2,1)} %bitcast.128), calls=%async_computation.16 | async-start | bytes 5767168 | tf_op jit(solution)/shard_map/all_to_all | solution.py:48
  444.5 18.1 %all-reduce.1 = (f32[1024]{0:T(1024)S(1)}, f32[128]{0:T(128)}, f32[128]{0:T(128)}, f32[1024]{0:T(1024)S(1)}) all-reduce(f32[1024]{0:T(1024)S(1)} %get-tuple-element.15, f32[128]{0:T(128)} %get-tuple-element.17, f32[128]{0:T(128)} %get-tuple-element.19, f32[1024]{0:T(1024)S(1)} %get-tuple-element.13), channel_id=1, replica_groups=mesh['row'=16,'col'=8] {'col'}, use_global_device_ids=true, to_apply=%region_19.20 | all-reduce | flops 2304 | bytes 18432 | tf_op jit(solution)/shard_map/psum | solution.py:283
  462.6 51.3 %all-reduce = (f32[1024]{0:T(1024)}, f32[128]{0:T(128)}, f32[128]{0:T(128)}, f32[1024]{0:T(1024)}) all-reduce(f32[1024]{0:T(1024)S(1)} %get-tuple-element.25, f32[128]{0:T(128)} %get-tuple-element.26, f32[128]{0:T(128)} %get-tuple-element.27, f32[1024]{0:T(1024)S(1)} %get-tuple-element.28), channel_id=1, replica_groups=mesh['row'=16,'col'=8] {'row'}, use_global_device_ids=true, to_apply=%region_20.21 | all-reduce | flops 2304 | bytes 18432 | tf_op jit(solution)/shard_map/psum | solution.py:282
  (321 shorter events, 252.2 us)
Async XLA Ops:
  0.6 27.0 %copy-start = (s32[2,512]{1,0:T(2,128)S(1)}, s32[2,512]{1,0:T(2,128)}, u32[]{:S(2)}) copy-start(s32[2,512]{1,0:T(2,128)} %param.20) | copy-start | bytes 12292
  0.7 13.1 %copy-start.58 = (bf16[2,512,128]{2,1,0:T(8,128)(2,1)S(1)}, bf16[2,512,128]{2,1,0:T(8,128)(2,1)}, u32[]{:S(2)}) copy-start(bf16[2,512,128]{2,1,0:T(8,128)(2,1)} %param.17) | copy-start | bytes 786436
  3.5 14.7 %all-to-all-start.3 = ((s32[16,2,32]{2,1,0:T(2,128)}), s32[16,2,32]{2,1,0:T(2,128)S(1)}, u32[]{:S(2)}, u32[]{:S(2)}) async-start(s32[16,2,32]{2,1,0:T(2,128)} %copy.266), calls=%async_computation.3 | async-start | bytes 32768 | tf_op jit(solution)/shard_map/all_to_all | solution.py:48
  14.6 13.1 %copy-start.56 = (bf16[1024]{0:T(1024)(128)(2,1)S(1)}, bf16[1024]{0:T(1024)(128)(2,1)}, u32[]{:S(2)}) copy-start(bf16[1024]{0:T(1024)(128)(2,1)} %param.21) | copy-start | bytes 6148
  14.6 13.1 %copy-start.49 = (bf16[384,64]{0,1:T(8,128)(2,1)S(1)}, bf16[384,64]{0,1:T(8,128)(2,1)}, u32[]{:S(2)}) copy-start(bf16[384,64]{0,1:T(8,128)(2,1)} %param.31) | copy-start | bytes 147460
  14.6 13.1 %copy-start.50 = (bf16[64,384]{1,0:T(8,128)(2,1)S(1)}, bf16[64,384]{1,0:T(8,128)(2,1)}, u32[]{:S(2)}) copy-start(bf16[64,384]{1,0:T(8,128)(2,1)} %param.30) | copy-start | bytes 147460
  14.6 13.1 %copy-start.51 = (bf16[64,384]{1,0:T(8,128)(2,1)S(1)}, bf16[64,384]{1,0:T(8,128)(2,1)}, u32[]{:S(2)}) copy-start(bf16[64,384]{1,0:T(8,128)(2,1)} %param.29) | copy-start | bytes 147460
  14.7 13.1 %copy-start.53 = (bf16[256,64]{0,1:T(8,128)(2,1)S(1)}, bf16[256,64]{0,1:T(8,128)(2,1)}, u32[]{:S(2)}) copy-start(bf16[256,64]{0,1:T(8,128)(2,1)} %param.27) | copy-start | bytes 98308
  19.4 21.2 %all-to-all-start.1 = ((bf16[16,64,512]{2,1,0:T(8,128)(2,1)}), bf16[16,64,512]{2,1,0:T(8,128)(2,1)S(1)}, u32[]{:S(2)}, u32[]{:S(2)}) async-start(bf16[16,64,512]{2,1,0:T(8,128)(2,1)} %broadcast_in_dim.59), calls=%async_computation.1 | async-start | bytes 2097152 | tf_op jit(solution)/shard_map/all_to_all | solution.py:48
  47.4 25.1 %all-to-all-start = ((bf16[128,32,128]{2,1,0:T(8,128)(2,1)}), bf16[128,32,128]{2,1,0:T(8,128)(2,1)S(1)}, u32[]{:S(2)}, u32[]{:S(2)}) async-start(bf16[128,32,128]{2,1,0:T(8,128)(2,1)} %bitcast.398), calls=%async_computation | async-start | bytes 2097152 | tf_op jit(solution)/shard_map/all_to_all | solution.py:48
  60.6 11.9 %copy-start.44 = (bf16[64,1408]{1,0:T(8,128)(2,1)S(1)}, bf16[64,1408]{1,0:T(8,128)(2,1)}, u32[]{:S(2)}) copy-start(bf16[64,1408]{1,0:T(8,128)(2,1)} %pad_maximum_fusion.5) | copy-start | bytes 540676
  74.4 46.4 %all-to-all-start.4 = ((bf16[16,64,1408]{2,1,0:T(8,128)(2,1)}), bf16[16,64,1408]{2,1,0:T(8,128)(2,1)}, u32[]{:S(2)}, u32[]{:S(2)}) async-start(bf16[16,64,1408]{2,1,0:T(8,128)(2,1)} %broadcast_in_dim.72), calls=%async_computation.4 | async-start | bytes 5767168 | tf_op jit(solution)/shard_map/all_to_all | solution.py:48
  134.1 30.5 %all-to-all-start.9 = ((bf16[128,32,128]{2,1,0:T(8,128)(2,1)}), bf16[128,32,128]{2,1,0:T(8,128)(2,1)S(1)}, u32[]{:S(2)}, u32[]{:S(2)}) async-start(bf16[128,32,128]{2,1,0:T(8,128)(2,1)} %bitcast.399), calls=%async_computation.9 | async-start | bytes 2097152 | tf_op jit(solution)/shard_map/all_to_all | solution.py:48
  164.7 20.0 %all-to-all-start.6 = ((bf16[4,512,2,128]{3,2,1,0:T(2,128)(2,1)}), bf16[4,512,2,128]{3,2,1,0:T(2,128)(2,1)}, u32[]{:S(2)}, u32[]{:S(2)}) async-start(bf16[4,512,2,128]{3,2,1,0:T(2,128)(2,1)} %bitcast.403), calls=%async_computation.6 | async-start | bytes 2097152 | tf_op jit(solution)/shard_map/all_to_all | solution.py:48
  189.9 26.4 %all-to-all-start.7 = ((bf16[4,512,2,128]{3,2,1,0:T(2,128)(2,1)}), bf16[4,512,2,128]{3,2,1,0:T(2,128)(2,1)}, u32[]{:S(2)}, u32[]{:S(2)}) async-start(bf16[4,512,2,128]{3,2,1,0:T(2,128)(2,1)} %broadcast_in_dim.74), calls=%async_computation.7 | async-start | bytes 2097152 | tf_op jit(solution)/shard_map/all_to_all | solution.py:48
  245.4 21.1 %all-to-all-start.10 = ((bf16[4,512,2,128]{3,2,1,0:T(2,128)(2,1)}), bf16[4,512,2,128]{3,2,1,0:T(2,128)(2,1)}, u32[]{:S(2)}, u32[]{:S(2)}) async-start(bf16[4,512,2,128]{3,2,1,0:T(2,128)(2,1)} %bitcast.404), calls=%async_computation.10 | async-start | bytes 2097152 | tf_op jit(solution)/shard_map/all_to_all | solution.py:48
  271.7 18.7 %all-to-all-start.11 = ((bf16[4,512,2,128]{3,2,1,0:T(2,128)(2,1)}), bf16[4,512,2,128]{3,2,1,0:T(2,128)(2,1)}, u32[]{:S(2)}, u32[]{:S(2)}) async-start(bf16[4,512,2,128]{3,2,1,0:T(2,128)(2,1)} %broadcast_in_dim.78), calls=%async_computation.11 | async-start | bytes 2097152 | tf_op jit(solution)/shard_map/all_to_all | solution.py:48
  328.8 11.9 %all-to-all-start.13 = ((bf16[2,8,2,64,512]{4,3,1,2,0:T(8,128)(2,1)}), bf16[2,8,2,64,512]{4,3,1,2,0:T(8,128)(2,1)}, u32[]{:S(2)}, u32[]{:S(2)}) async-start(bf16[2,8,2,64,512]{4,3,1,2,0:T(8,128)(2,1)} %copy.301), calls=%async_computation.13 | async-start | bytes 4194304 | tf_op jit(solution)/shard_map/all_to_all | solution.py:48
  340.7 30.2 %all-to-all-start.8 = ((bf16[128,32,128]{2,1,0:T(8,128)(2,1)}), bf16[128,32,128]{2,1,0:T(8,128)(2,1)S(1)}, u32[]{:S(2)}, u32[]{:S(2)}) async-start(bf16[128,32,128]{2,1,0:T(8,128)(2,1)} %bitcast.400), calls=%async_computation.8 | async-start | bytes 2097152 | tf_op jit(solution)/shard_map/all_to_all | solution.py:48
  370.9 14.6 %copy-start.17 = (bf16[128,32,128]{2,1,0:T(8,128)(2,1)}, bf16[128,32,128]{2,1,0:T(8,128)(2,1)S(1)}, u32[]{:S(2)}) copy-start(bf16[128,32,128]{2,1,0:T(8,128)(2,1)S(1)} %all-to-all-done.8) | copy-start | bytes 3145732
  385.5 24.2 %all-to-all-start.14 = ((bf16[16,64,512]{2,1,0:T(8,128)(2,1)}), bf16[16,64,512]{2,1,0:T(8,128)(2,1)S(1)}, u32[]{:S(2)}, u32[]{:S(2)}) async-start(bf16[16,64,512]{2,1,0:T(8,128)(2,1)} %bitcast.114), calls=%async_computation.14 | async-start | bytes 2097152 | tf_op jit(solution)/shard_map/all_to_all | solution.py:48
  409.7 10.0 %copy-start.20 = (bf16[16,64,512]{2,1,0:T(8,128)(2,1)}, bf16[16,64,512]{2,1,0:T(8,128)(2,1)S(1)}, u32[]{:S(2)}) copy-start(bf16[16,64,512]{2,1,0:T(8,128)(2,1)S(1)} %all-to-all-done.14) | copy-start | bytes 3145732
  409.7 24.8 %all-to-all-start.12 = ((bf16[128,32,128]{2,1,0:T(8,128)(2,1)}), bf16[128,32,128]{2,1,0:T(8,128)(2,1)S(1)}, u32[]{:S(2)}, u32[]{:S(2)}) async-start(bf16[128,32,128]{2,1,0:T(8,128)(2,1)} %bitcast.97), calls=%async_computation.12 | async-start | bytes 2097152 | tf_op jit(solution)/shard_map/all_to_all | solution.py:48
  435.5 83.3 %all-to-all-start.16 = ((bf16[16,64,1408]{2,1,0:T(8,128)(2,1)}), bf16[16,64,1408]{2,1,0:T(8,128)(2,1)S(1)}, u32[]{:S(2)}, u32[]{:S(2)}) async-start(bf16[16,64,1408]{2,1,0:T(8,128)(2,1)} %bitcast.128), calls=%async_computation.16 | async-start | bytes 5767168 | tf_op jit(solution)/shard_map/all_to_all | solution.py:48
  (59 other events, 185.6 us)
